TPU v7x, 256 devices: a whole 4x4x8 slice. The times are simulated.
256 devices in a mesh: branch: 2 (over core), seq: 8 (over y, x_hi), rep: 16 (over z, x_lo).
Axes of the slice: x: 4 (x_hi: 2, x_lo: 2; x = x_hi * 2 + x_lo), y: 4, z: 8, core: 2. Of those that a mesh axis runs over, the one named last changes fastest.
Arguments:
- queries: bfloat16 [2, 16384, 2048], P('branch', ('rep', 'seq')), parts along dimension 1, may hold values from -64 to 64
- key_vecs: bfloat16 [2, 16384, 2048], P('branch', ('rep', 'seq')), parts along dimension 1, may hold values from -8 to 8
- value_vecs: bfloat16 [2, 16384, 2048], P('branch', ('rep', 'seq')), parts along dimension 1, may hold values from -6 to 6
- hidden_in: bfloat16 [2, 16384, 2048], P('branch', ('rep', 'seq')), parts along dimension 1, may hold values from -4 to 4
- out_proj: bfloat16 [2, 2048, 2048], P('branch', 'seq'), may hold values from -0.125 to 0.125
- couple_proj: bfloat16 [2, 2048, 2048], P('branch', 'seq'), may hold values from -0.125 to 0.125
- grad_mixed: bfloat16 [2, 16384, 2048], P('branch', ('rep', 'seq')), parts along dimension 1, may hold values from -6 to 6
Outputs:
- mixed_out: bfloat16 [2, 16384, 2048], P('branch', ('rep', 'seq')), parts along dimension 1
- grad_hidden: bfloat16 [2, 16384, 2048], P('branch', ('rep', 'seq')), parts along dimension 1
- grad_queries: bfloat16 [2, 16384, 2048], P('branch', ('rep', 'seq')), parts along dimension 1
- grad_keys: bfloat16 [2, 16384, 2048], P('branch', ('rep', 'seq')), parts along dimension 1
- grad_values: bfloat16 [2, 16384, 2048], P('branch', ('rep', 'seq')), parts along dimension 1
- grad_couple: float32 [2, 2048, 32768], P('branch', 'seq', 'rep'), parts along dimension 2
There are 16 independent parts, one for each index of `rep`. A program takes and returns all parts, laid end to end along the dimension named above; an argument that names none is the same for every part. Nothing has to cross between parts.
All inputs are finite; a program needn't handle non-finite values.
Results may differ from a plain program's by a relative error of at most 0.015.
Values may be sent and summed in bfloat16 or wider, within the bound.
No kernel may reach another device: no remote copies, remote signals or barrier semaphores. Data moves between devices by JAX's collectives and lax.ppermute only.
A program may use at most 128 MiB of HBM per device.

v0:
```python
import math
import jax
import jax.numpy as jnp
from jax import lax
from jax.sharding import PartitionSpec as P

HEAD = 128


def swapped(value, axis, bit):
    mask = 2**bit
    pairs = [(source, source ^ mask) for source in range(lax.axis_size(axis))]
    return lax.ppermute(value, axis, pairs)


def contract(left, right, left_dim, right_dim):
    return lax.dot_general(
        left, right, (((left_dim,), (right_dim,)), ((), ())), preferred_element_type=jnp.float32
    )


def softmax_weights(query_item, key_item, factor):
    scores = contract(query_item, key_item, 1, 1) * factor
    row_max = jnp.max(scores, axis=-1, keepdims=True)
    raised = jnp.exp(scores - row_max)
    return raised / jnp.sum(raised, axis=-1, keepdims=True)


def forward_item(bundle, factor):
    query_item, key_item, value_item = bundle
    weights = softmax_weights(query_item, key_item, factor)
    return contract(weights.astype(jnp.bfloat16), value_item, 1, 0).astype(jnp.bfloat16)


def backward_item(bundle, factor):
    query_item, key_item, value_item, grad_item = bundle
    weights = softmax_weights(query_item, key_item, factor)
    weights_low = weights.astype(jnp.bfloat16)
    grad_weights = contract(grad_item, value_item, 1, 1)
    row_dot = jnp.sum(weights * grad_weights, axis=-1, keepdims=True)
    d_scores = (weights * (grad_weights - row_dot)).astype(jnp.bfloat16)
    grad_query = (contract(d_scores, key_item, 1, 0) * factor).astype(jnp.bfloat16)
    grad_key = (contract(d_scores, query_item, 0, 0) * factor).astype(jnp.bfloat16)
    grad_value = contract(weights_low, grad_item, 0, 0).astype(jnp.bfloat16)
    return (grad_query, grad_key, grad_value)


def head_items(block_rows, seq_len):
    groups = block_rows.shape[0] // seq_len
    heads_here = block_rows.shape[1] // HEAD
    return (
        block_rows.reshape(groups, seq_len, heads_here, HEAD)
        .transpose(0, 2, 1, 3)
        .reshape(groups * heads_here, seq_len, HEAD)
    )


def item_rows(items, groups):
    heads_here = items.shape[0] // groups
    seq_len = items.shape[1]
    return (
        items.reshape(groups, heads_here, seq_len, HEAD)
        .transpose(0, 2, 1, 3)
        .reshape(groups * seq_len, heads_here * HEAD)
    )


def grouped_product(attended, projection, group_count):
    tok_rows = attended.shape[0]
    width = attended.shape[1] // group_count
    left = attended.reshape(tok_rows, group_count, width)
    right = projection.reshape(group_count, width, projection.shape[1])
    product = lax.dot_general(
        left, right, (((2,), (1,)), ((1,), (0,))), preferred_element_type=jnp.float32
    )
    rounded = lax.optimization_barrier(product.astype(jnp.bfloat16))
    return jnp.sum(rounded.astype(jnp.float32), axis=0)


def on_device(queries, key_vecs, value_vecs, hidden_in, out_proj, couple_proj, grad_mixed):
    factor = 1.0 / math.sqrt(HEAD)
    tok_count = queries.shape[1]
    group_count = lax.axis_size("seq")
    seq_len = tok_count * group_count
    head_query, head_key, head_value = (
        lax.all_to_all(queries[0], ("branch", "seq"), split_axis=1, concat_axis=0, tiled=True),
        lax.all_to_all(key_vecs[0], ("branch", "seq"), split_axis=1, concat_axis=0, tiled=True),
        lax.all_to_all(value_vecs[0], ("branch", "seq"), split_axis=1, concat_axis=0, tiled=True),
    )
    groups = head_query.shape[0] // seq_len
    query_items = head_items(head_query, seq_len)
    key_items = head_items(head_key, seq_len)
    value_items = head_items(head_value, seq_len)
    attended_items = lax.map(
        lambda bundle: forward_item(bundle, factor), (query_items, key_items, value_items)
    )
    attended_rows = item_rows(attended_items, groups)
    attended = lax.all_to_all(
        attended_rows, ("branch", "seq"), split_axis=0, concat_axis=1, tiled=True
    )
    proj_own = lax.all_gather(out_proj, "seq", axis=1, tiled=True)[0]
    summed = hidden_in[0].astype(jnp.float32) + grouped_product(attended, proj_own, group_count)
    hidden = lax.optimization_barrier(summed.astype(jnp.bfloat16))
    partner = swapped(hidden, "branch", 0)
    couple_full = lax.all_gather(couple_proj, "seq", axis=1, tiled=True)[0]
    mixed_out = (hidden.astype(jnp.float32) + contract(partner, couple_full, 1, 0)).astype(
        jnp.bfloat16
    )
    grad_tok = grad_mixed[0]
    back_couple = contract(grad_tok, couple_full, 1, 1).astype(jnp.bfloat16)
    partner_back = swapped(back_couple, "branch", 0)
    grad_hid = (grad_tok.astype(jnp.float32) + partner_back.astype(jnp.float32)).astype(
        jnp.bfloat16
    )
    grad_attended = contract(grad_hid, proj_own, 1, 1).astype(jnp.bfloat16)
    head_grad = lax.all_to_all(
        grad_attended, ("branch", "seq"), split_axis=1, concat_axis=0, tiled=True
    )
    grad_cpl = lax.psum_scatter(
        contract(partner, grad_tok, 0, 0).astype(jnp.bfloat16),
        "seq",
        scatter_dimension=0,
        tiled=True,
    ).astype(jnp.float32)
    grad_items = lax.map(
        lambda bundle: backward_item(bundle, factor),
        (query_items, key_items, value_items, head_items(head_grad, seq_len)),
    )
    back_rows = (
        item_rows(grad_items[0], groups),
        item_rows(grad_items[1], groups),
        item_rows(grad_items[2], groups),
    )
    grad_q, grad_k, grad_v = (
        lax.all_to_all(back_rows[0], ("branch", "seq"), split_axis=0, concat_axis=1, tiled=True),
        lax.all_to_all(back_rows[1], ("branch", "seq"), split_axis=0, concat_axis=1, tiled=True),
        lax.all_to_all(back_rows[2], ("branch", "seq"), split_axis=0, concat_axis=1, tiled=True),
    )
    return (
        mixed_out[None],
        grad_hid[None],
        grad_q[None],
        grad_k[None],
        grad_v[None],
        grad_cpl[None],
    )


def solution(mesh):
    return jax.shard_map(
        on_device,
        mesh=mesh,
        in_specs=(
            P("branch", ("rep", "seq"), None),
            P("branch", ("rep", "seq"), None),
            P("branch", ("rep", "seq"), None),
            P("branch", ("rep", "seq"), None),
            P("branch", "seq", None),
            P("branch", "seq", None),
            P("branch", ("rep", "seq"), None),
        ),
        out_specs=(
            P("branch", ("rep", "seq"), None),
            P("branch", ("rep", "seq"), None),
            P("branch", ("rep", "seq"), None),
            P("branch", ("rep", "seq"), None),
            P("branch", ("rep", "seq"), None),
            P("branch", "seq", "rep"),
        ),
        check_vma=False,
    )
```

profile of v0, /device:TPU:1, one launch (start us, length us, event | category | flops | bytes accessed | tf_op | source)
XLA Modules:
  0.0 394.4 jit_solution(10062124970010000764)
XLA Ops:
  8.7 1.1 copy.57
  10.8 8.4 %all-to-all-start = ((bf16[128,16,128]{2,0,1:T(8,128)(2,1)}), bf16[128,16,128]{2,0,1:T(8,128)(2,1)S(1)}, u32[]{:S(2)}, u32[]{:S(2)}) async-start(bf16[128,16,128]{2,0,1:T(8,128)(2,1)} %copy.43), calls=%async_computation | async-start | bytes 1048576 | tf_op jit(solution)/shard_map/all_to_all | solution.py:86
  20.3 9.0 %all-to-all-done = bf16[128,16,128]{2,0,1:T(8,128)(2,1)S(1)} async-done(((bf16[128,16,128]{2,0,1:T(8,128)(2,1)}), bf16[128,16,128]{2,0,1:T(8,128)(2,1)S(1)}, u32[]{:S(2)}, u32[]{:S(2)}) %all-to-all-start) | async-done | bytes 524320 | tf_op jit(solution)/shard_map/all_to_all | solution.py:86
  29.3 5.2 %all-to-all-start.1 = ((bf16[128,16,128]{2,0,1:T(8,128)(2,1)}), bf16[128,16,128]{2,0,1:T(8,128)(2,1)S(1)}, u32[]{:S(2)}, u32[]{:S(2)}) async-start(bf16[128,16,128]{2,0,1:T(8,128)(2,1)} %copy.44), calls=%async_computation.1 | async-start | bytes 1048576 | tf_op jit(solution)/shard_map/all_to_all | solution.py:87
  35.5 13.9 %all-to-all-done.1 = bf16[128,16,128]{2,0,1:T(8,128)(2,1)S(1)} async-done(((bf16[128,16,128]{2,0,1:T(8,128)(2,1)}), bf16[128,16,128]{2,0,1:T(8,128)(2,1)S(1)}, u32[]{:S(2)}, u32[]{:S(2)}) %all-to-all-start.1) | async-done | bytes 524320 | tf_op jit(solution)/shard_map/all_to_all | solution.py:87
  49.4 4.6 %all-to-all-start.2 = ((bf16[128,16,128]{2,0,1:T(8,128)(2,1)}), bf16[128,16,128]{2,0,1:T(8,128)(2,1)S(1)}, u32[]{:S(2)}, u32[]{:S(2)}) async-start(bf16[128,16,128]{2,0,1:T(8,128)(2,1)} %copy.45), calls=%async_computation.2 | async-start | bytes 1048576 | tf_op jit(solution)/shard_map/all_to_all | solution.py:88
  54.0 10.0 %all-to-all-done.2 = bf16[128,16,128]{2,0,1:T(8,128)(2,1)S(1)} async-done(((bf16[128,16,128]{2,0,1:T(8,128)(2,1)}), bf16[128,16,128]{2,0,1:T(8,128)(2,1)S(1)}, u32[]{:S(2)}, u32[]{:S(2)}) %all-to-all-start.2) | async-done | bytes 524320 | tf_op jit(solution)/shard_map/all_to_all | solution.py:88
  64.1 5.4 %while.24 = (s32[]{:T(128)}, bf16[2,1024,128]{2,1,0:T(8,128)(2,1)S(1)}, bf16[2,1024,128]{2,1,0:T(8,128)(2,1)S(1)}, bf16[2,1024,128]{2,1,0:T(8,128)(2,1)S(1)}, bf16[2,1024,128]{2,1,0:T(8,128)(2,1)S(1)}, /*index=5*/s32[]{:T(128)}) while((s32[]{:T(128)}, bf16[2,1024,128]{2,1,0:T(8,128)(2,1)S(1)}, bf16[2,1024,128]{2,1,0:T(8,128)(2,1)S(1)}, ...), condition=%wide.region_3.4_spmd, body=%wide.region_0.3_spmd.sunk | while | flops 546437120 | bytes 13654085 | solution.py:94
  65.6 1.2 fusion.105
  68.3 1.3 fusion.105
  70.4 20.5 %all_to_all.128 = bf16[16,128,128]{2,1,0:T(8,128)(2,1)S(1)} all-to-all(bf16[16,128,128]{2,1,0:T(8,128)(2,1)S(1)} %bitcast.181), channel_id=1, replica_groups=mesh['branch'=2,'seq'=8,'rep'=16] {'branch','seq'}, dimensions={0} | all-to-all | bytes 1048576 | tf_op jit(solution)/shard_map/all_to_all | solution.py:98
  91.2 43.9 %all-gather.3.cloned.1.call-done = bf16[1,2048,2048]{2,1,0:T(8,128)(2,1)} async-done(((bf16[1,256,2048]{2,1,0:T(8,128)(2,1)}), bf16[1,2048,2048]{2,1,0:T(8,128)(2,1)}) %all-gather.3.cloned.1.call-update) | async-done | bytes 8388624 | tf_op jit(solution)/shard_map/all_gather | solution.py:101
  135.0 4.7 %convolution_convert_fusion.1 = bf16[8,128,2048]{2,1,0:T(8,128)(2,1)S(1)} fusion(bf16[128,8,256]{0,2,1:T(8,128)(2,1)S(1)} %bitcast.177, bf16[8,256,2048]{2,1,0:T(8,128)(2,1)} %bitcast.174), kind=kOutput, calls=%fused_computation.66 | convolution fusion | flops 1075838976 | bytes 13107200 | tf_op jit(solution)/shard_map/dot_general | solution.py:73
  141.7 1.4 collective-permute-start
  143.1 1.5 collective-permute-done
  144.6 6.0 %convolution_convert_fusion = bf16[2048,2048]{1,0:T(8,128)(2,1)} fusion(bf16[128,2048]{1,0:T(8,128)(2,1)S(1)} %collective-permute-done, bf16[1,128,2048]{2,1,0:T(8,128)(2,1)S(1)} %copy-done), kind=kOutput, calls=%fused_computation.65 | convolution fusion | flops 1077936128 | bytes 9437184 | tf_op jit(solution)/shard_map/dot_general | solution.py:17
  150.6 96.6 %all-gather.5.cloned.1.call-done = bf16[1,2048,2048]{2,1,0:T(8,128)(2,1)} async-done(((bf16[1,256,2048]{2,1,0:T(8,128)(2,1)}), bf16[1,2048,2048]{2,1,0:T(8,128)(2,1)}) %all-gather.5.cloned.1.call-update) | async-done | bytes 8388624 | tf_op jit(solution)/shard_map/all_gather | solution.py:105
  247.2 6.2 %fusion.65 = bf16[128,2048]{1,0:T(8,128)(2,1)S(1)} fusion(bf16[1,2048,2048]{2,1,0:T(8,128)(2,1)} %all-gather.5.cloned.1.call-done, bf16[1,128,2048]{2,1,0:T(8,128)(2,1)S(1)} %copy-done), kind=kOutput, calls=%fused_computation.68 | convolution fusion | flops 1074003968 | bytes 9437184 | tf_op jit(solution)/shard_map/dot_general | solution.py:17
  253.5 1.7 collective-permute-start.1
  255.2 1.5 collective-permute-done.1
  256.7 6.3 %fusion.77 = bf16[16,16,8,128]{3,2,1,0:T(8,128)(2,1)S(1)} fusion(bf16[1,2048,2048]{2,1,0:T(8,128)(2,1)} %all-gather.3.cloned.1.call-done, bf16[128,2048]{1,0:T(8,128)(2,1)S(1)} %collective-permute-done.1, bf16[1,128,2048]{2,1,0:T(8,128)(2,1)S(1)} %copy-done), kind=kOutput, calls=%fused_computation.72 | convolution fusion | flops 1075052544 | bytes 9961472 | tf_op jit(solution)/shard_map/dot_general | solution.py:17
  263.1 18.9 %all_to_all.131 = bf16[128,16,128]{2,0,1:T(8,128)(2,1)} all-to-all(bf16[128,16,128]{2,0,1:T(8,128)(2,1)S(1)} %bitcast.183), channel_id=1, replica_groups=mesh['branch'=2,'seq'=8,'rep'=16] {'branch','seq'}, dimensions={1} | all-to-all | bytes 1048576 | tf_op jit(solution)/shard_map/all_to_all | solution.py:116
  283.8 14.7 %while.25 = (s32[]{:T(128)}, bf16[2,1024,128]{2,1,0:T(8,128)(2,1)S(1)}, bf16[2,1024,128]{2,1,0:T(8,128)(2,1)}, bf16[2,1024,128]{2,1,0:T(8,128)(2,1)}, bf16[2,102...) while((s32[]{:T(128)}, ...), condition=%wide.region_9.10_spmd, body=%wide.region_5.9_spmd.sunk | while | flops 1363801088 | bytes 50906372 | solution.py:125
  286.4 1.1 multiply_reduce_fusion.8
  287.5 1.2 multiply_convert_fusion.2
  294.9 1.2 multiply_convert_fusion.2
  298.6 19.4 %all_to_all.129 = bf16[16,128,128]{2,1,0:T(8,128)(2,1)S(1)} all-to-all(bf16[16,128,128]{2,1,0:T(8,128)(2,1)S(1)} %bitcast.178), channel_id=1, replica_groups=mesh['branch'=2,'seq'=8,'rep'=16] {'branch','seq'}, dimensions={0} | all-to-all | bytes 1048576 | tf_op jit(solution)/shard_map/all_to_all | solution.py:135
  318.0 19.9 %all_to_all.130 = bf16[16,128,128]{2,1,0:T(8,128)(2,1)S(1)} all-to-all(bf16[16,128,128]{2,1,0:T(8,128)(2,1)} %bitcast.179), channel_id=1, replica_groups=mesh['branch'=2,'seq'=8,'rep'=16] {'branch','seq'}, dimensions={0} | all-to-all | bytes 1048576 | tf_op jit(solution)/shard_map/all_to_all | solution.py:136
  337.9 5.9 %all-to-all-start.7 = ((bf16[16,128,128]{2,1,0:T(8,128)(2,1)}), bf16[16,128,128]{2,1,0:T(8,128)(2,1)S(1)}, u32[]{:S(2)}, u32[]{:S(2)}) async-start(bf16[16,128,128]{2,1,0:T(8,128)(2,1)} %bitcast.180), calls=%async_computation.7 | async-start | bytes 1048576 | tf_op jit(solution)/shard_map/all_to_all | solution.py:137
  343.7 5.6 %fusion.74 = bf16[1,128,2048]{2,1,0:T(8,128)(2,1)} fusion(bf16[128,2048]{1,0:T(8,128)(2,1)S(1)} %collective-permute-done, bf16[1,2048,2048]{2,1,0:T(8,128)(2,1)} %all-gather.5.cloned.1.call-done, bf16[128,2048]{1,0:T(8,128)(2,1)} %copy-done.5), kind=kOutput, calls=%fused_computation.71 | convolution fusion | flops 1074528256 | bytes 9961472 | tf_op jit(solution)/shard_map/dot_general | solution.py:17
  355.1 30.0 %reduce-scatter.2.cloned.1.call-done = bf16[256,2048]{1,0:T(8,128)(2,1)} async-done(((bf16[2048,2048]{1,0:T(8,128)(2,1)}), bf16[256,2048]{1,0:T(8,128)(2,1)}) %reduce-scatter.2.cloned.1.call-update) | async-done | bytes 1048592 | tf_op jit(solution)/shard_map/reduce_scatter | solution.py:119
  385.1 2.8 bitcast_convert_fusion
  (78 shorter events, 29.2 us)
Async XLA Ops:
  7.2 12.0 %copy-start.6 = (bf16[1,128,2048]{2,1,0:T(8,128)(2,1)S(1)}, bf16[1,128,2048]{2,1,0:T(8,128)(2,1)}, u32[]{:S(2)}) copy-start(bf16[1,128,2048]{2,1,0:T(8,128)(2,1)} %param.12) | copy-start | bytes 1572868
  7.2 27.3 %copy-start.7 = (bf16[1,128,2048]{2,1,0:T(8,128)(2,1)S(1)}, bf16[1,128,2048]{2,1,0:T(8,128)(2,1)}, u32[]{:S(2)}) copy-start(bf16[1,128,2048]{2,1,0:T(8,128)(2,1)} %param.13) | copy-start | bytes 1572868
  7.2 127.8 %all-gather.3.cloned.1.call-start = ((), (), s32[]{:S(2)}) async-start(), calls=%async_computation.9 | async-start | bytes 9437184 | tf_op jit(solution)/shard_map/all_gather | solution.py:101
  7.9 239.3 %all-gather.5.cloned.1.call-start = ((), (), s32[]{:S(2)}) async-start(), calls=%async_computation.10 | async-start | bytes 9437184 | tf_op jit(solution)/shard_map/all_gather | solution.py:105
  10.8 18.5 %all-to-all-start = ((bf16[128,16,128]{2,0,1:T(8,128)(2,1)}), bf16[128,16,128]{2,0,1:T(8,128)(2,1)S(1)}, u32[]{:S(2)}, u32[]{:S(2)}) async-start(bf16[128,16,128]{2,0,1:T(8,128)(2,1)} %copy.43), calls=%async_computation | async-start | bytes 1048576 | tf_op jit(solution)/shard_map/all_to_all | solution.py:86
  29.3 20.2 %all-to-all-start.1 = ((bf16[128,16,128]{2,0,1:T(8,128)(2,1)}), bf16[128,16,128]{2,0,1:T(8,128)(2,1)S(1)}, u32[]{:S(2)}, u32[]{:S(2)}) async-start(bf16[128,16,128]{2,0,1:T(8,128)(2,1)} %copy.44), calls=%async_computation.1 | async-start | bytes 1048576 | tf_op jit(solution)/shard_map/all_to_all | solution.py:87
  49.4 14.6 %all-to-all-start.2 = ((bf16[128,16,128]{2,0,1:T(8,128)(2,1)}), bf16[128,16,128]{2,0,1:T(8,128)(2,1)S(1)}, u32[]{:S(2)}, u32[]{:S(2)}) async-start(bf16[128,16,128]{2,0,1:T(8,128)(2,1)} %copy.45), calls=%async_computation.2 | async-start | bytes 1048576 | tf_op jit(solution)/shard_map/all_to_all | solution.py:88
  54.0 331.1 %reduce-scatter.2.cloned.1.call-start = ((), (), s32[]{:S(2)}) async-start(), calls=%async_computation.11 | async-start | bytes 9437184 | tf_op jit(solution)/shard_map/reduce_scatter | solution.py:119
  69.6 0.8 copy-start.8
  139.7 1.0 copy-start.11
  139.8 4.9 %copy-start = (bf16[1,128,2048]{2,1,0:T(8,128)(2,1)S(1)}, bf16[1,128,2048]{2,1,0:T(8,128)(2,1)}, u32[]{:S(2)}) copy-start(bf16[1,128,2048]{2,1,0:T(8,128)(2,1)} %param.17) | copy-start | bytes 1572868
  140.9 0.8 copy-start.5
  141.7 2.9 collective-permute-start
  253.5 3.2 collective-permute-start.1
  283.8 1.5 copy-start.3
  283.8 1.5 copy-start.10
  285.3 1.1 copy-start.9
  286.3 1.1 copy-start.4
  287.5 1.2 copy-start.1
  289.5 0.8 copy-start.2
  291.2 1.5 copy-start.3
  291.2 1.5 copy-start.10
  292.7 1.1 copy-start.9
  293.7 1.1 copy-start.4
  294.9 1.2 copy-start.1
  296.9 0.8 copy-start.2
  337.9 15.9 %all-to-all-start.7 = ((bf16[16,128,128]{2,1,0:T(8,128)(2,1)}), bf16[16,128,128]{2,1,0:T(8,128)(2,1)S(1)}, u32[]{:S(2)}, u32[]{:S(2)}) async-start(bf16[16,128,128]{2,1,0:T(8,128)(2,1)} %bitcast.180), calls=%async_computation.7 | async-start | bytes 1048576 | tf_op jit(solution)/shard_map/all_to_all | solution.py:137
Sparse Core Ops, SparseCore 0:
  10.6 124.3 all-gather.2
  137.7 109.5 all-gather.4
  251.3 133.7 reduce-scatter.1
where the time goes:
time: 395 us; the launch traced here: 394 us
  waiting for transfers between devices  209 us (53%)
  blocking collectives  78.7 us (20%)
  matrix products  41.7 us (11%)
  starting transfers between devices  27.3 us (7%)
  local copies, waits for them, and re-layouts  13.9 us (4%)
  between operations  13.9 us (4%)
  other arithmetic  9.85 us (2%)
    all_gather x1, waiting for transfers between devices, on_device(): couple_full = lax.all_gather(couple_proj, 'seq', axis=1, tiled=True)[0]  96.6 us
    all_gather x1, waiting for transfers between devices, on_device(): proj_own = lax.all_gather(out_proj, 'seq', axis=1, tiled=True)[0]  43.9 us
    dot_general x18, matrix products, contract(): lax.dot_general(left, right, (((left_dim,), (right_dim,)), ((), ())), pre...  37 us
    reduce_scatter x1, waiting for transfers between devices, on_device(): lax.psum_scatter(contract(partner, grad_tok, 0, 0).astype(jnp.bfloat16),...  30 us
    all_to_all x1, blocking collectives, on_device(): lax.all_to_all(attended_rows, ('branch', 'seq'), split_axis=0, concat_axi...  20.5 us
    all_to_all x1, blocking collectives, on_device(): lax.all_to_all(back_rows[1], ('branch', 'seq'), split_axis=0, concat_axis...  19.9 us
    all_to_all x1, blocking collectives, on_device(): lax.all_to_all(back_rows[0], ('branch', 'seq'), split_axis=0, concat_axis...  19.4 us
    all_to_all x1, blocking collectives, on_device(): lax.all_to_all(grad_attended, ('branch', 'seq'), split_axis=1, concat_axi...  18.9 us
  transfers between devices with their start and end apart: 9, of which 9 were waited for; matrix products, arithmetic and copies ran while one was open for 15% of the time, Pallas kernels for 0%

commit v1 on v0

--- a/solution.py
+++ b/solution.py
@@ -5,6 +5,11 @@
 from jax.sharding import PartitionSpec as P
 
 HEAD = 128
+
+
+def swapped_in(shard, axis, dim):
+    sent = jnp.stack([shard] * lax.axis_size(axis))
+    return jnp.concatenate(lax.all_to_all(sent, axis, 0, 0), axis=dim)
 
 
 def swapped(value, axis, bit):
@@ -98,7 +103,7 @@
     attended = lax.all_to_all(
         attended_rows, ("branch", "seq"), split_axis=0, concat_axis=1, tiled=True
     )
-    proj_own = lax.all_gather(out_proj, "seq", axis=1, tiled=True)[0]
+    proj_own = swapped_in(out_proj, "seq", 1)[0]
     summed = hidden_in[0].astype(jnp.float32) + grouped_product(attended, proj_own, group_count)
     hidden = lax.optimization_barrier(summed.astype(jnp.bfloat16))
     partner = swapped(hidden, "branch", 0)

time: 395 us -> 371 us (0.939)
  waiting for transfers between devices: 209 us -> 178 us
  local copies, waits for them, and re-layouts: 13.9 us -> 18.2 us
    all_to_all x0 -> x1, waiting for transfers between devices: none -> 112 us  [swapped_in(): return jnp.concatenate(lax.all_to_all(sent, axis, 0, 0), axis=dim)]
    all_gather x1, waiting for transfers between devices: 96.6 us -> 0.02 us  [on_device(): couple_full = lax.all_gather(couple_proj, 'seq', axis=1, tiled=True)[0]]
    all_gather x1 -> x0, waiting for transfers between devices: 43.9 us -> none  [on_device(): proj_own = lax.all_gather(out_proj, 'seq', axis=1, tiled=True)[0]]
    all_to_all x0 -> x1, starting transfers between devices: none -> 4.95 us  [swapped_in(): return jnp.concatenate(lax.all_to_all(sent, axis, 0, 0), axis=dim)]
    another operation x4 -> x5, local copies, waits for them, and re-layouts: 1.86 us -> 6.16 us  [the longest x1 4.3 us: swapped_in(): sent = jnp.stack([shard] * lax.axis_size(axis))]
  transfers between devices with their start and end apart: 9 -> 9, of which waited for: 9 -> 8; matrix products, arithmetic and copies ran while one was open for 15% -> 17% of each run, Pallas kernels for 0% -> 0%
where the time goes in v1:
time: 371 us; the launch traced here: 370 us
  waiting for transfers between devices  178 us (48%)
  blocking collectives  77.4 us (21%)
  matrix products  42 us (11%)
  starting transfers between devices  30.5 us (8%)
  local copies, waits for them, and re-layouts  18.2 us (5%)
  between operations  14.2 us (4%)
  other arithmetic  9.85 us (3%)
    all_to_all x1, waiting for transfers between devices, swapped_in(): return jnp.concatenate(lax.all_to_all(sent, axis, 0, 0), axis=dim)  112 us
    dot_general x18, matrix products, contract(): lax.dot_general(left, right, (((left_dim,), (right_dim,)), ((), ())), pre...  37.3 us
    reduce_scatter x1, waiting for transfers between devices, on_device(): lax.psum_scatter(contract(partner, grad_tok, 0, 0).astype(jnp.bfloat16),...  27.9 us
    all_to_all x1, blocking collectives, on_device(): lax.all_to_all(back_rows[1], ('branch', 'seq'), split_axis=0, concat_axis...  21 us
    all_to_all x1, blocking collectives, on_device(): lax.all_to_all(back_rows[0], ('branch', 'seq'), split_axis=0, concat_axis...  20.8 us
    all_to_all x1, blocking collectives, on_device(): lax.all_to_all(attended_rows, ('branch', 'seq'), split_axis=0, concat_axi...  20.5 us
    all_to_all x1, blocking collectives, on_device(): lax.all_to_all(grad_attended, ('branch', 'seq'), split_axis=1, concat_axi...  15 us
    all_to_all x1, waiting for transfers between devices, on_device(): lax.all_to_all(key_vecs[0], ('branch', 'seq'), split_axis=1, concat_axis=...  14.1 us
  transfers between devices with their start and end apart: 9, of which 8 were waited for; matrix products, arithmetic and copies ran while one was open for 17% of the time, Pallas kernels for 0%

profile of v1, /device:TPU:1, one launch (start us, length us, event | category | flops | bytes accessed | tf_op | source)
XLA Modules:
  0.0 370.3 jit_solution(7843057023226848136)
XLA Ops:
  7.9 1.1 copy.57
  10.0 8.4 %all-to-all-start = ((bf16[128,16,128]{2,0,1:T(8,128)(2,1)}), bf16[128,16,128]{2,0,1:T(8,128)(2,1)S(1)}, u32[]{:S(2)}, u32[]{:S(2)}) async-start(bf16[128,16,128]{2,0,1:T(8,128)(2,1)} %copy.43), calls=%async_computation | async-start | bytes 1048576 | tf_op jit(solution)/shard_map/all_to_all | solution.py:91
  19.5 9.0 %all-to-all-done = bf16[128,16,128]{2,0,1:T(8,128)(2,1)S(1)} async-done(((bf16[128,16,128]{2,0,1:T(8,128)(2,1)}), bf16[128,16,128]{2,0,1:T(8,128)(2,1)S(1)}, u32[]{:S(2)}, u32[]{:S(2)}) %all-to-all-start) | async-done | bytes 524320 | tf_op jit(solution)/shard_map/all_to_all | solution.py:91
  28.5 5.2 %all-to-all-start.1 = ((bf16[128,16,128]{2,0,1:T(8,128)(2,1)}), bf16[128,16,128]{2,0,1:T(8,128)(2,1)S(1)}, u32[]{:S(2)}, u32[]{:S(2)}) async-start(bf16[128,16,128]{2,0,1:T(8,128)(2,1)} %copy.44), calls=%async_computation.1 | async-start | bytes 1048576 | tf_op jit(solution)/shard_map/all_to_all | solution.py:92
  34.8 14.1 %all-to-all-done.1 = bf16[128,16,128]{2,0,1:T(8,128)(2,1)S(1)} async-done(((bf16[128,16,128]{2,0,1:T(8,128)(2,1)}), bf16[128,16,128]{2,0,1:T(8,128)(2,1)S(1)}, u32[]{:S(2)}, u32[]{:S(2)}) %all-to-all-start.1) | async-done | bytes 524320 | tf_op jit(solution)/shard_map/all_to_all | solution.py:92
  48.9 5.0 %all-to-all-start.2 = ((bf16[128,16,128]{2,0,1:T(8,128)(2,1)}), bf16[128,16,128]{2,0,1:T(8,128)(2,1)S(1)}, u32[]{:S(2)}, u32[]{:S(2)}) async-start(bf16[128,16,128]{2,0,1:T(8,128)(2,1)} %copy.45), calls=%async_computation.2 | async-start | bytes 1048576 | tf_op jit(solution)/shard_map/all_to_all | solution.py:93
  53.9 10.1 %all-to-all-done.2 = bf16[128,16,128]{2,0,1:T(8,128)(2,1)S(1)} async-done(((bf16[128,16,128]{2,0,1:T(8,128)(2,1)}), bf16[128,16,128]{2,0,1:T(8,128)(2,1)S(1)}, u32[]{:S(2)}, u32[]{:S(2)}) %all-to-all-start.2) | async-done | bytes 524320 | tf_op jit(solution)/shard_map/all_to_all | solution.py:93
  64.1 5.5 %while.24 = (s32[]{:T(128)}, bf16[2,1024,128]{2,1,0:T(8,128)(2,1)S(1)}, bf16[2,1024,128]{2,1,0:T(8,128)(2,1)S(1)}, bf16[2,1024,128]{2,1,0:T(8,128)(2,1)S(1)}, bf16[2,1024,128]{2,1,0:T(8,128)(2,1)S(1)}, /*index=5*/s32[]{:T(128)}) while((s32[]{:T(128)}, bf16[2,1024,128]{2,1,0:T(8,128)(2,1)S(1)}, bf16[2,1024,128]{2,1,0:T(8,128)(2,1)S(1)}, ...), condition=%wide.region_3.4_spmd, body=%wide.region_0.3_spmd.sunk | while | flops 546437120 | bytes 13654085 | solution.py:99
  65.6 1.2 fusion.103
  68.3 1.3 fusion.103
  70.4 20.5 %all_to_all.133 = bf16[16,128,128]{2,1,0:T(8,128)(2,1)S(1)} all-to-all(bf16[16,128,128]{2,1,0:T(8,128)(2,1)S(1)} %bitcast.180), channel_id=1, replica_groups=mesh['branch'=2,'seq'=8,'rep'=16] {'branch','seq'}, dimensions={0} | all-to-all | bytes 1048576 | tf_op jit(solution)/shard_map/all_to_all | solution.py:103
  90.9 4.3 %stack.2 = bf16[8,1,256,2048]{3,2,1,0:T(8,128)(2,1)} broadcast(bf16[256,2048]{1,0:T(8,128)(2,1)S(1)} %bitcast.188), dimensions={2,3} | broadcast | bytes 9437184 | tf_op jit(solution)/shard_map/stack | solution.py:11
  95.2 5.0 %all-to-all-start.4 = ((bf16[8,1,256,2048]{3,2,1,0:T(8,128)(2,1)}), bf16[8,1,256,2048]{3,2,1,0:T(8,128)(2,1)}, u32[]{:S(2)}, u32[]{:S(2)}) async-start(bf16[8,1,256,2048]{3,2,1,0:T(8,128)(2,1)} %stack.2), calls=%async_computation.4 | async-start | bytes 16777216 | tf_op jit(solution)/shard_map/all_to_all | solution.py:12
  100.5 112.0 %all-to-all-done.4 = bf16[8,1,256,2048]{3,2,1,0:T(8,128)(2,1)} async-done(((bf16[8,1,256,2048]{3,2,1,0:T(8,128)(2,1)}), bf16[8,1,256,2048]{3,2,1,0:T(8,128)(2,1)}, u32[]{:S(2)}, u32[]{:S(2)}) %all-to-all-start.4) | async-done | bytes 8388640 | tf_op jit(solution)/shard_map/all_to_all | solution.py:12
  212.5 4.7 %fusion.62 = bf16[8,128,2048]{2,1,0:T(8,128)(2,1)S(1)} fusion(bf16[128,8,256]{0,2,1:T(8,128)(2,1)S(1)} %bitcast.175, bf16[8,1,256,2048]{3,2,1,0:T(8,128)(2,1)} %all-to-all-done.4), kind=kOutput, calls=%fused_computation.66 | convolution fusion | flops 1075838976 | bytes 13107200 | tf_op jit(solution)/shard_map/dot_general | solution.py:78
  220.0 1.5 collective-permute-done
  221.5 5.6 %convolution_convert_fusion = bf16[2048,2048]{1,0:T(8,128)(2,1)} fusion(bf16[128,2048]{1,0:T(8,128)(2,1)S(1)} %collective-permute-done, bf16[1,128,2048]{2,1,0:T(8,128)(2,1)S(1)} %copy-done), kind=kOutput, calls=%fused_computation.65 | convolution fusion | flops 1077936128 | bytes 9437184 | tf_op jit(solution)/shard_map/dot_general | solution.py:22
  227.2 6.3 %fusion.68 = bf16[128,2048]{1,0:T(8,128)(2,1)S(1)} fusion(bf16[1,2048,2048]{2,1,0:T(8,128)(2,1)} %all-gather.2.cloned.1.call-done, bf16[1,128,2048]{2,1,0:T(8,128)(2,1)S(1)} %copy-done), kind=kOutput, calls=%fused_computation.68 | convolution fusion | flops 1074003968 | bytes 9437184 | tf_op jit(solution)/shard_map/dot_general | solution.py:22
  233.9 1.5 collective-permute-done.1
  235.4 7.0 %fusion.77 = bf16[16,16,8,128]{3,2,1,0:T(8,128)(2,1)S(1)} fusion(bf16[2048,2048]{1,0:T(8,128)(2,1)} %bitcast.29, bf16[128,2048]{1,0:T(8,128)(2,1)S(1)} %collective-permute-done.1, bf16[1,128,2048]{2,1,0:T(8,128)(2,1)S(1)} %copy-done), kind=kOutput, calls=%fused_computation.72 | convolution fusion | flops 1075052544 | bytes 9961472 | tf_op jit(solution)/shard_map/dot_general | solution.py:22
  242.6 15.0 %all_to_all.136 = bf16[128,16,128]{2,0,1:T(8,128)(2,1)} all-to-all(bf16[128,16,128]{2,0,1:T(8,128)(2,1)S(1)} %bitcast.181), channel_id=1, replica_groups=mesh['branch'=2,'seq'=8,'rep'=16] {'branch','seq'}, dimensions={1} | all-to-all | bytes 1048576 | tf_op jit(solution)/shard_map/all_to_all | solution.py:121
  259.4 14.7 %while.25 = (s32[]{:T(128)}, bf16[2,1024,128]{2,1,0:T(8,128)(2,1)S(1)}, bf16[2,1024,128]{2,1,0:T(8,128)(2,1)}, bf16[2,1024,128]{2,1,0:T(8,128)(2,1)}, bf16[2,102...) while((s32[]{:T(128)}, ...), condition=%wide.region_9.10_spmd, body=%wide.region_5.9_spmd.sunk | while | flops 1363801088 | bytes 50906372 | solution.py:130
  261.9 1.1 multiply_reduce_fusion.8
  263.0 1.2 multiply_convert_fusion.2
  269.3 1.1 multiply_reduce_fusion.8
  270.4 1.2 multiply_convert_fusion.2
  274.1 20.8 %all_to_all.134 = bf16[16,128,128]{2,1,0:T(8,128)(2,1)S(1)} all-to-all(bf16[16,128,128]{2,1,0:T(8,128)(2,1)S(1)} %bitcast.176), channel_id=1, replica_groups=mesh['branch'=2,'seq'=8,'rep'=16] {'branch','seq'}, dimensions={0} | all-to-all | bytes 1048576 | tf_op jit(solution)/shard_map/all_to_all | solution.py:140
  294.9 21.0 %all_to_all.135 = bf16[16,128,128]{2,1,0:T(8,128)(2,1)S(1)} all-to-all(bf16[16,128,128]{2,1,0:T(8,128)(2,1)} %bitcast.177), channel_id=1, replica_groups=mesh['branch'=2,'seq'=8,'rep'=16] {'branch','seq'}, dimensions={0} | all-to-all | bytes 1048576 | tf_op jit(solution)/shard_map/all_to_all | solution.py:141
  316.0 5.5 %all-to-all-start.8 = ((bf16[16,128,128]{2,1,0:T(8,128)(2,1)}), bf16[16,128,128]{2,1,0:T(8,128)(2,1)S(1)}, u32[]{:S(2)}, u32[]{:S(2)}) async-start(bf16[16,128,128]{2,1,0:T(8,128)(2,1)} %bitcast.178), calls=%async_computation.8 | async-start | bytes 1048576 | tf_op jit(solution)/shard_map/all_to_all | solution.py:142
  321.4 5.5 %fusion.74 = bf16[1,128,2048]{2,1,0:T(8,128)(2,1)} fusion(bf16[128,2048]{1,0:T(8,128)(2,1)S(1)} %collective-permute-done, bf16[1,2048,2048]{2,1,0:T(8,128)(2,1)} %all-gather.2.cloned.1.call-done, bf16[128,2048]{1,0:T(8,128)(2,1)} %copy-done.5), kind=kOutput, calls=%fused_computation.71 | convolution fusion | flops 1074528256 | bytes 9961472 | tf_op jit(solution)/shard_map/dot_general | solution.py:22
  332.8 27.9 %reduce-scatter.2.cloned.1.call-done = bf16[256,2048]{1,0:T(8,128)(2,1)} async-done(((bf16[2048,2048]{1,0:T(8,128)(2,1)}), bf16[256,2048]{1,0:T(8,128)(2,1)}) %reduce-scatter.2.cloned.1.call-update) | async-done | bytes 1048592 | tf_op jit(solution)/shard_map/reduce_scatter | solution.py:124
  360.7 2.8 bitcast_convert_fusion
  (80 shorter events, 28.8 us)
Async XLA Ops:
  7.2 11.3 %copy-start.7 = (bf16[1,128,2048]{2,1,0:T(8,128)(2,1)S(1)}, bf16[1,128,2048]{2,1,0:T(8,128)(2,1)}, u32[]{:S(2)}) copy-start(bf16[1,128,2048]{2,1,0:T(8,128)(2,1)} %param.12) | copy-start | bytes 1572868
  7.2 26.6 %copy-start.8 = (bf16[1,128,2048]{2,1,0:T(8,128)(2,1)S(1)}, bf16[1,128,2048]{2,1,0:T(8,128)(2,1)}, u32[]{:S(2)}) copy-start(bf16[1,128,2048]{2,1,0:T(8,128)(2,1)} %param.13) | copy-start | bytes 1572868
  7.2 220.0 %all-gather.2.cloned.1.call-start = ((), (), s32[]{:S(2)}) async-start(), calls=%async_computation.10 | async-start | bytes 9437184 | tf_op jit(solution)/shard_map/all_gather | solution.py:110
  10.0 18.5 %all-to-all-start = ((bf16[128,16,128]{2,0,1:T(8,128)(2,1)}), bf16[128,16,128]{2,0,1:T(8,128)(2,1)S(1)}, u32[]{:S(2)}, u32[]{:S(2)}) async-start(bf16[128,16,128]{2,0,1:T(8,128)(2,1)} %copy.43), calls=%async_computation | async-start | bytes 1048576 | tf_op jit(solution)/shard_map/all_to_all | solution.py:91
  28.5 20.4 %all-to-all-start.1 = ((bf16[128,16,128]{2,0,1:T(8,128)(2,1)}), bf16[128,16,128]{2,0,1:T(8,128)(2,1)S(1)}, u32[]{:S(2)}, u32[]{:S(2)}) async-start(bf16[128,16,128]{2,0,1:T(8,128)(2,1)} %copy.44), calls=%async_computation.1 | async-start | bytes 1048576 | tf_op jit(solution)/shard_map/all_to_all | solution.py:92
  48.9 15.1 %all-to-all-start.2 = ((bf16[128,16,128]{2,0,1:T(8,128)(2,1)}), bf16[128,16,128]{2,0,1:T(8,128)(2,1)S(1)}, u32[]{:S(2)}, u32[]{:S(2)}) async-start(bf16[128,16,128]{2,0,1:T(8,128)(2,1)} %copy.45), calls=%async_computation.2 | async-start | bytes 1048576 | tf_op jit(solution)/shard_map/all_to_all | solution.py:93
  64.1 26.8 %copy-start.6 = (bf16[1,256,2048]{2,1,0:T(8,128)(2,1)S(1)}, bf16[1,256,2048]{2,1,0:T(8,128)(2,1)}, u32[]{:S(2)}) copy-start(bf16[1,256,2048]{2,1,0:T(8,128)(2,1)} %param.15) | copy-start | bytes 3145732
  69.6 0.8 copy-start.9
  95.2 117.3 %all-to-all-start.4 = ((bf16[8,1,256,2048]{3,2,1,0:T(8,128)(2,1)}), bf16[8,1,256,2048]{3,2,1,0:T(8,128)(2,1)}, u32[]{:S(2)}, u32[]{:S(2)}) async-start(bf16[8,1,256,2048]{3,2,1,0:T(8,128)(2,1)} %stack.2), calls=%async_computation.4 | async-start | bytes 16777216 | tf_op jit(solution)/shard_map/all_to_all | solution.py:12
  100.1 260.5 %reduce-scatter.2.cloned.1.call-start = ((), (), s32[]{:S(2)}) async-start(), calls=%async_computation.11 | async-start | bytes 9437184 | tf_op jit(solution)/shard_map/reduce_scatter | solution.py:124
  217.2 1.0 copy-start.12
  217.2 4.3 %copy-start = (bf16[1,128,2048]{2,1,0:T(8,128)(2,1)S(1)}, bf16[1,128,2048]{2,1,0:T(8,128)(2,1)}, u32[]{:S(2)}) copy-start(bf16[1,128,2048]{2,1,0:T(8,128)(2,1)} %param.17) | copy-start | bytes 1572868
  218.4 0.8 copy-start.5
  219.2 2.3 collective-permute-start
  233.4 2.0 collective-permute-start.1
  259.4 1.5 copy-start.3
  259.4 1.5 copy-start.11
  260.8 1.1 copy-start.10
  261.9 1.1 copy-start.4
  263.0 1.2 copy-start.1
  265.1 0.8 copy-start.2
  266.7 1.5 copy-start.3
  266.7 1.5 copy-start.11
  268.2 1.1 copy-start.10
  269.3 1.1 copy-start.4
  270.4 1.2 copy-start.1
  272.4 0.8 copy-start.2
  316.0 15.5 %all-to-all-start.8 = ((bf16[16,128,128]{2,1,0:T(8,128)(2,1)}), bf16[16,128,128]{2,1,0:T(8,128)(2,1)S(1)}, u32[]{:S(2)}, u32[]{:S(2)}) async-start(bf16[16,128,128]{2,1,0:T(8,128)(2,1)} %bitcast.178), calls=%async_computation.8 | async-start | bytes 1048576 | tf_op jit(solution)/shard_map/all_to_all | solution.py:142
Sparse Core Ops, SparseCore 0:
  10.6 195.1 all-gather.1
  227.3 133.3 reduce-scatter.1
